TPU v7x, 256 devices: a whole 4x4x8 slice. The times are simulated.
256 devices in a mesh: wide: 64 (over x, z, core), narrow: 4 (over y).
Axes of the slice: x: 4, y: 4, z: 8, core: 2. Of those that a mesh axis runs over, the one named last changes fastest.
Arguments:
- dosage: bfloat16 [262144, 4096], P(('wide', 'narrow')), may hold values from 0 to 2
- keep_rows: int32 [229376], P(('wide', 'narrow')), may hold values from 0 to 1023, as said below
- allele_counts: int32 [4096], replicated, may hold values from 157286 to 367000, as said below
- projection: bfloat16 [4096, 128], replicated, may hold values from -0.09375 to 0.09375
Outputs:
- scores: float32 [229376, 128], P(('wide', 'narrow'))
- loadings: float32 [4096, 128], P('narrow')
Inputs may be any that keep to these rules, and one draw needn't show every extreme that they name: `keep_rows`: each block of 896 entries holds distinct local row numbers of one device's 1024 samples, ascending. `allele_counts`: totals over all 262144 genotyped samples, before outlier removal.
All inputs are finite; a program needn't handle non-finite values.
Results may differ from a plain program's by a relative error of at most 0.0075.
The roundings to bfloat16 on the way count: a program that leaves them out, or rounds other values in their place, can miss the bound.
Values sent between devices are 32-bit elements; how exact they have to be, the bound alone decides.
A program may use at most 64 MiB of HBM per device.

v0:
```python
import math

import jax
import jax.numpy as jnp
from jax import lax
from jax.sharding import PartitionSpec as P

ITERS = 2


def transposed_product(left_side, right_side):
    return lax.dot_general(
        left_side, right_side, (((0,), (0,)), ((), ())), preferred_element_type=jnp.float32
    )


def invert_factor(gram_matrix):
    lower_factor = jnp.linalg.cholesky(gram_matrix)
    unit_matrix = jnp.eye(gram_matrix.shape[0], dtype=jnp.float32)
    return jax.scipy.linalg.solve_triangular(lower_factor, unit_matrix, lower=True)


def on_device(dosage, keep_rows, allele_counts, projection):
    groups = lax.axis_size("wide") * lax.axis_size("narrow")
    samples_total = dosage.shape[0] * groups
    kept_total = keep_rows.shape[0] * groups
    snp_count = dosage.shape[1]
    narrow_size = lax.axis_size("narrow")
    share_rows = snp_count // narrow_size
    position = lax.axis_index("narrow")
    frequency = allele_counts.astype(jnp.float32) / (2.0 * samples_total)
    center = 2.0 * frequency
    spread = jnp.sqrt(2.0 * frequency * (1.0 - frequency))
    chosen = jnp.take(dosage, keep_rows, axis=0)
    standard = ((chosen.astype(jnp.float32) - center) / spread).astype(jnp.bfloat16)
    projected = jnp.dot(standard, projection, preferred_element_type=jnp.float32).astype(
        jnp.bfloat16
    )
    inverse = None
    loadings = None
    for iteration in range(ITERS):
        last_turn = iteration + 1 == ITERS
        gram_matrix = None
        gram_matrix = lax.psum(transposed_product(projected, projected), ("wide", "narrow"))
        totals = lax.psum(transposed_product(standard, projected), ("wide", "narrow"))
        inverse = invert_factor(gram_matrix)
        loadings_all = jnp.dot(totals, inverse.T, precision=lax.Precision.HIGHEST)
        if last_turn:
            loadings = lax.dynamic_slice_in_dim(loadings_all, position * share_rows, share_rows, 0)
        else:
            projected = jnp.dot(
                standard, loadings_all.astype(jnp.bfloat16), preferred_element_type=jnp.float32
            ).astype(jnp.bfloat16)
    scores = jnp.dot(
        projected.astype(jnp.float32), inverse.T, precision=lax.Precision.HIGHEST
    ) * math.sqrt(kept_total)
    return (scores, loadings)


def solution(mesh):
    in_specs = (P(("wide", "narrow"), None), P(("wide", "narrow")), P(), P())
    out_specs = (P(("wide", "narrow"), None), P("narrow", None))
    return jax.shard_map(
        on_device, mesh=mesh, in_specs=in_specs, out_specs=out_specs, check_vma=False
    )
```

profile of v0, /device:TPU:8, one launch (start us, length us, event | category | flops | bytes accessed | tf_op | source)
XLA Modules:
  0.0 645.3 jit_solution(8097715273102711557)
XLA Ops:
  7.2 0.8 compare_select_fusion
  8.0 0.7 compare_and_fusion
  8.7 0.7 convert_multiply_fusion
  9.4 19.5 %gather_fusion = bf16[896,4096]{1,0:T(8,128)(2,1)} fusion(bf16[1024,4096]{1,0:T(8,128)(2,1)} %param.7, s32[1024]{0:T(1024)S(1)} %pad_clamp_fusion), kind=kCustom, calls=%fused_computation | custom fusion | bytes 14683648 | tf_op jit(solution)/shard_map/jit(_take)/gather | solution.py:34
  28.9 6.6 %divide_convert_fusion = bf16[896,4096]{1,0:T(8,128)(2,1)S(1)} fusion(f32[4096]{0:T(1024)S(1)} %get-tuple-element.9, f32[4096]{0:T(1024)S(1)} %get-tuple-element.8, bf16[896,4096]{1,0:T(8,128)(2,1)} %gather_fusion, pred[896]{0:T(1024)(128)(4,1)S(1)} %compare_and_fusion), kind=kLoop, calls=%fused_computation.1 | loop fusion | flops 18350080 | bytes 14713728 | tf_op jit(solution)/shard_map/convert_element_type | solution.py:35
  35.5 2.1 convolution_convert_fusion.2
  37.6 3.5 fusion.10
  41.1 0.9 fusion.11
  42.0 0.2 all-reduce.5.cloned.1.call-start
  42.3 266.6 %all-reduce.7.cloned.1.call-done = (f32[4096,128]{1,0:T(8,128)}, f32[128,128]{0,1:T(8,128)}) async-done(((f32[4096,128]{1,0:T(8,128)}, f32[128,128]{0,1:T(8,128)}), (f32[4096,128]{1,0:T(8,128)}, f32[128,128]{0,1:T(8,128)})) %all-reduce.7.cloned.1.call-update) | async-done | bytes 2162704 | tf_op jit(solution)/shard_map/psum | solution.py:45
  308.9 0.9 copy.7
  309.8 0.9 fusion.9
  310.6 11.7 %cholesky.44 = f32[128,128]{1,0:T(8,128)S(1)} custom-call(f32[128,128]{1,0:T(8,128)S(1)} %fusion.9), custom_call_target="Cholesky" | custom-call | tf_op jit(solution)/shard_map/jit(cholesky)/cholesky | solution.py:18
  322.4 0.6 compare_reduce_fusion.1
  323.0 0.7 fusion.4
  323.7 9.8 %custom-call.6 = f32[1,128,128]{1,2,0:T(8,128)S(1)} custom-call(f32[1,128,128]{2,1,0:T(8,128)S(1)} %fusion.4), custom_call_target="InvertDiagBlocksLowerTriangular" | custom-call | tf_op jit(solution)/shard_map/jit(_solve_triangular)/triangular_solve | solution.py:20
  333.5 0.3 fusion.2
  333.8 3.5 convolution_convert_fusion
  337.4 5.3 convolution_convert_fusion.1
  342.7 3.5 fusion.13
  346.2 0.9 fusion.12
  347.1 260.8 %all-reduce.5.cloned.1.call-done = (f32[128,128]{0,1:T(8,128)}, f32[4096,128]{1,0:T(8,128)}) async-done(((f32[128,128]{0,1:T(8,128)}, f32[4096,128]{1,0:T(8,128)}), (f32[128,128]{0,1:T(8,128)}, f32[4096,128]{1,0:T(8,128)})) %all-reduce.5.cloned.1.call-update) | async-done | bytes 2162704 | tf_op jit(solution)/shard_map/psum | solution.py:44
  607.9 1.1 copy.9
  609.0 0.9 fusion.7
  609.9 11.7 %cholesky.55 = f32[128,128]{1,0:T(8,128)S(1)} custom-call(f32[128,128]{1,0:T(8,128)S(1)} %fusion.7), custom_call_target="Cholesky" | custom-call | tf_op jit(solution)/shard_map/jit(cholesky)/cholesky | solution.py:18
  621.6 0.6 compare_reduce_fusion
  622.3 0.7 fusion.5
  623.0 9.8 %custom-call.7 = f32[1,128,128]{1,2,0:T(8,128)S(1)} custom-call(f32[1,128,128]{2,1,0:T(8,128)S(1)} %fusion.5), custom_call_target="InvertDiagBlocksLowerTriangular" | custom-call | tf_op jit(solution)/shard_map/jit(_solve_triangular)/triangular_solve | solution.py:20
  632.8 0.3 fusion
  633.1 1.1 convolution_multiply_fusion
  634.2 3.5 fusion.14
  637.7 0.8 constant_dynamic-slice_fusion
  (15 shorter events, 0.2 us)
Async XLA Ops:
  7.2 28.3 %copy-start = (bf16[4096,128]{1,0:T(8,128)(2,1)S(1)}, bf16[4096,128]{1,0:T(8,128)(2,1)}, u32[]{:S(2)}) copy-start(bf16[4096,128]{1,0:T(8,128)(2,1)} %param.10) | copy-start | bytes 3145732
  7.2 301.7 %all-reduce.7.cloned.1.call-start = ((), (), s32[]{:S(2)}) async-start(), calls=%async_computation.1 | async-start | bytes 4325376 | tf_op jit(solution)/shard_map/psum | solution.py:45
  35.5 5.6 copy-start.1
  42.0 565.9 %all-reduce.5.cloned.1.call-start = ((), (), s32[]{:S(2)}) async-start(), calls=%async_computation | async-start | bytes 4325376 | tf_op jit(solution)/shard_map/psum | solution.py:44
  333.8 8.9 %slice-start = ((s8[7340032]{0:T(1024)(128)(4,1)}), s8[4194304]{0:T(1024)(128)(4,1)S(1)}, s32[]{:S(2)}) async-start(s8[7340032]{0:T(1024)(128)(4,1)} %bitcast.36), calls=%async_computation.2 | async-start | bytes 8388608
  337.4 5.3 slice-start.1
Sparse Core Ops, SparseCore 0:
  42.2 266.6 all-reduce.6
  347.3 260.5 all-reduce.4
where the time goes:
time: 646 us; the launch traced here: 645 us
  waiting for transfers between devices  527 us (82%)
  other arithmetic  56.2 us (9%)
  matrix products  24.9 us (4%)
  local copies, waits for them, and re-layouts  22.4 us (3%)
  between operations  14.2 us (2%)
    psum x1, waiting for transfers between devices, on_device(): lax.psum(transposed_product(standard, projected), ('wide', 'narrow'))  267 us
    psum x1, waiting for transfers between devices, on_device(): lax.psum(transposed_product(projected, projected), ('wide', 'narrow'))  261 us
    another operation x6, other arithmetic, invert_factor(): lower_factor = jnp.linalg.cholesky(gram_matrix)  24.8 us
    another operation x4, other arithmetic, invert_factor(): jax.scipy.linalg.solve_triangular(lower_factor, unit_matrix, lower=True)  20.9 us
    gather x1, local copies, waits for them, and re-layouts, on_device(): chosen = jnp.take(dosage, keep_rows, axis=0)  19.5 us
  transfers between devices with their start and end apart: 2, of which 2 were waited for; matrix products, arithmetic and copies ran while one was open for 0% of the time, Pallas kernels for 0%

commit v1 on v0

v1 whole, which is shorter than its diff:
```python
import math

import jax
import jax.numpy as jnp
from jax import lax
from jax.experimental import pallas as pl
from jax.experimental.pallas import tpu as pltpu
from jax.sharding import PartitionSpec as P

ITERS = 2
NX, NY, NZ = 4, 4, 8
COMP = 128
SLAB = 512
MESH = pl.DeviceIdType.MESH
HIGH = lax.Precision.HIGHEST

PER_ITER = 46


def kernel(
    samples_total,
    kept_total,
    dosage_hbm,
    keep_ref,
    counts_ref,
    proj_ref,
    scores_ref,
    load_ref,
    stand,
    acc,
    pm,
    pt,
    mask,
    wt,
    core_in,
    chip_sum,
    first_in,
    first_sum,
    second_in,
    second_sum,
    third_in,
    whole,
    basis_t,
    gram,
    gram_core,
    gram_half,
    gram_x,
    gram_y,
    gram_z,
    gram_all,
    elim,
    unit,
    inv_t,
    kept,
    load_sem,
    send_sem,
    recv_sem,
):
    wide = lax.axis_index("wide")
    y = lax.axis_index("narrow")
    c = lax.rem(wide, 2)
    z = lax.rem(lax.div(wide, 2), NZ)
    x = lax.div(wide, 2 * NZ)
    f = x * (1 - c) + y * c
    s = y * (1 - c) + x * c

    def at(px, py, pz, pc):
        return ((px * NZ + pz) * 2 + pc, py)

    partner = at(x, y, z, 1 - c)

    def along_x(k):
        return at(lax.rem(x + k, NX), y, z, c)

    def along_y(k):
        return at(x, lax.rem(y + k, NY), z, c)

    def along_z(k):
        return at(x, y, lax.rem(z + k, NZ), c)

    def along_f(k):
        return at(lax.rem(x + k * (1 - c), NX), lax.rem(y + k * c, NY), z, c)

    def along_s(k):
        return at(lax.rem(x + k * c, NX), lax.rem(y + k * (1 - c), NY), z, c)

    snps = stand.shape[1]
    slabs = snps // SLAB

    loads = []
    for i in range(slabs):
        part = pl.ds(i * SLAB, SLAB)
        loads.append(
            pltpu.make_async_copy(
                dosage_hbm.at[:, part], stand.at[:, part], load_sem.at[i]
            )
        )
        loads[-1].start()

    barrier = pltpu.get_barrier_semaphore()
    others = (
        [partner]
        + [along_x(k) for k in range(1, NX)]
        + [along_y(k) for k in range(1, NY)]
        + [along_z(k) for k in range(1, NZ)]
    )
    for other in others:
        pl.semaphore_signal(barrier, inc=1, device_id=other, device_id_type=MESH)

    keep_row = keep_ref[...]
    rows = stand.shape[0]
    n_kept = keep_row.shape[1]

    @pl.loop(0, rows // 128)
    def _(i):
        ids = lax.broadcasted_iota(jnp.int32, (128, n_kept), 0) + i * 128
        hit = jnp.max(
            jnp.where(ids == keep_row, 1.0, 0.0), axis=1, keepdims=True
        )
        mask[pl.ds(i * 128, 128), :] = jnp.broadcast_to(hit, (128, COMP))

    frequency = counts_ref[...].astype(jnp.float32) / (2.0 * samples_total)
    center = 2.0 * frequency
    scale = 1.0 / jnp.sqrt(2.0 * frequency * (1.0 - frequency))

    for i in range(slabs):
        loads[i].wait()
        part = slice(i * SLAB, (i + 1) * SLAB)
        mid = center[:, part]
        mul = scale[:, part]

        @pl.loop(0, rows // 64)
        def _(r):
            here = pl.ds(r * 64, 64)
            raw = stand[here, part].astype(jnp.float32)
            stand[here, part] = ((raw - mid) * mul).astype(jnp.bfloat16)

        term = jnp.dot(
            stand[:, part], proj_ref[part, :], preferred_element_type=jnp.float32
        )
        if i == 0:
            acc[...] = term
        else:
            acc[...] += term

    pl.semaphore_wait(barrier, len(others))

    sent = []
    count = [0]

    def send(src, dst, device):
        copy = pltpu.make_async_remote_copy(
            src_ref=src,
            dst_ref=dst,
            send_sem=send_sem.at[count[0]],
            recv_sem=recv_sem.at[count[0]],
            device_id=device,
            device_id_type=MESH,
        )
        count[0] += 1
        copy.start()
        sent.append(copy)
        return copy

    def arrive(copies):
        for copy in copies:
            copy.wait_recv()

    def eliminate(low, high):
        @pl.loop(low, high)
        def _(j):
            lane = lax.broadcasted_iota(jnp.int32, (COMP, COMP), 1)
            sub = lax.broadcasted_iota(jnp.int32, (COMP, 1), 0)
            lane_row = lax.broadcasted_iota(jnp.int32, (1, COMP), 1)
            now = elim[...]
            column = jnp.sum(jnp.where(lane == j, now, 0.0), axis=1, keepdims=True)
            row = elim[pl.ds(j, 1), :]
            unit_row = unit[pl.ds(j, 1), :]
            pivot = jnp.sum(
                jnp.where(lane_row == j, row, 0.0), axis=1, keepdims=True
            )
            factor = jnp.where(sub > j, column / pivot, 0.0)
            elim[...] = now - factor * row
            unit[...] = unit[...] - factor * unit_row

    for t in range(ITERS):
        last = t + 1 == ITERS
        wt_t, core_t, chip_t = wt.at[t], core_in.at[t], chip_sum.at[t]
        whole_t = whole.at[t]

        @pl.loop(0, rows // 128)
        def _(i):
            here = pl.ds(pl.multiple_of(i * 128, 128), 128)
            value = jnp.where(mask[here, :] > 0.0, acc[here, :], 0.0)
            pm[here, :] = value.astype(jnp.bfloat16)
            pt[:, here] = value.T.astype(jnp.bfloat16)

        gram[t] = jnp.dot(pt[...], pm[...], preferred_element_type=jnp.float32)
        g_core = send(gram.at[t], gram_core.at[t], partner)

        def partial_of(which):
            @pl.loop(0, NY)
            def _(i):
                start = pl.multiple_of(i * (snps // NY) + which * SLAB, SLAB)
                value = jnp.dot(
                    pt[...],
                    stand[:, pl.ds(start, SLAB)],
                    preferred_element_type=jnp.float32,
                )
                for j in range(NX):
                    pf = j * (1 - which) + i * which
                    ps = i * (1 - which) + j * which
                    wt_t[which, pf, ps] = value[:, j * 128 : (j + 1) * 128]

        partial_of(1 - c)
        core = send(wt_t.at[1 - c], core_t, partner)

        arrive([g_core])
        half = pl.ds(pl.multiple_of(c * 64, 64), 64)
        gram_half[t] = gram[t, half, :] + gram_core[t, half, :]
        g_x = []
        for k in range(1, NX):
            to = lax.rem(x + k, NX)
            g_x.append(
                send(
                    gram_half.at[t, pl.ds(pl.multiple_of(to * 16, 16), 16), :],
                    gram_x.at[t, x],
                    along_x(k),
                )
            )
        gram_x[t, x] = gram_half[t, pl.ds(pl.multiple_of(x * 16, 16), 16), :]

        partial_of(c)
        arrive([core])
        for i in range(4):

            @pl.loop(0, 4)
            def _(j):
                chip_t[i, j] = wt_t[c, i, j] + core_t[i, j]

        first = []
        for k in range(1, 4):
            to = lax.rem(f + k, 4)
            first.append(send(chip_t.at[to], first_in.at[t, k - 1], along_f(k)))

        arrive(g_x)
        gram_y[t, y] = (
            (gram_x[t, 0] + gram_x[t, 1]) + gram_x[t, 2]
        ) + gram_x[t, 3]
        g_y = [
            send(gram_y.at[t, y], gram_y.at[t, y], along_y(k)) for k in range(1, NY)
        ]
        arrive(g_y)
        gram_z[t, z] = (
            (gram_y[t, 0] + gram_y[t, 1]) + gram_y[t, 2]
        ) + gram_y[t, 3]
        g_z = [
            send(gram_z.at[t, z], gram_z.at[t, z], along_z(k)) for k in range(1, NZ)
        ]

        arrive(first)

        @pl.loop(0, 4)
        def _(j):
            first_sum[t, j] = (
                (chip_t[f, j] + first_in[t, 0, j]) + first_in[t, 1, j]
            ) + first_in[t, 2, j]

        second = []
        for k in range(1, 4):
            to = lax.rem(s + k, 4)
            second.append(
                send(first_sum.at[t, to], second_in.at[t, k - 1], along_s(k))
            )

        arrive(g_z)
        total = gram_z[t, 0]
        for k in range(1, NZ):
            total = total + gram_z[t, k]
        mine = pl.ds(pl.multiple_of(c * 64 + x * 16, 16), 16)
        gram_all[t, mine, :] = total
        g_xa = [
            send(gram_all.at[t, mine, :], gram_all.at[t, mine, :], along_x(k))
            for k in range(1, NX)
        ]

        arrive(second)
        second_sum[t] = (
            (first_sum[t, s] + second_in[t, 0]) + second_in[t, 1]
        ) + second_in[t, 2]
        third = []
        for k in range(1, NZ):
            to = lax.rem(z + k, NZ)
            third.append(
                send(
                    second_sum.at[t, pl.ds(pl.multiple_of(to * 16, 16), 16), :],
                    third_in.at[t, k - 1],
                    along_z(k),
                )
            )

        arrive(g_xa)
        g_ca = send(gram_all.at[t, half, :], gram_all.at[t, half, :], partner)
        arrive([g_ca])
        elim[...] = gram_all[t]
        unit[...] = jnp.where(
            lax.broadcasted_iota(jnp.int32, (COMP, COMP), 0)
            == lax.broadcasted_iota(jnp.int32, (COMP, COMP), 1),
            1.0,
            0.0,
        )

        arrive(third)
        piece = pl.ds(pl.multiple_of(z * 16, 16), 16)
        own = second_sum[t, piece, :]
        for k in range(1, NZ):
            own = own + third_in[t, k - 1]
        whole_t[c, f, s, piece, :] = own
        out_z = [
            send(
                whole_t.at[c, f, s, piece, :],
                whole_t.at[c, f, s, piece, :],
                along_z(k),
            )
            for k in range(1, NZ)
        ]
        eliminate(0, 40)
        arrive(out_z)
        block = whole_t.at[c, f, s]
        if not last:
            out_s = [send(block, block, along_s(k)) for k in range(1, 4)]
            eliminate(40, 72)
            arrive(out_s)
            band = whole_t.at[c, f]
            out_f = [send(band, band, along_f(k)) for k in range(1, 4)]
            eliminate(72, 128)
            arrive(out_f)
            out_c = send(whole_t.at[c], whole_t.at[c], partner)
        else:
            out_s = [send(block, block, along_x(k)) for k in range(1, 4)]
            eliminate(40, 72)
            arrive(out_s)
            out_c = None

        if last:
            pairs = []
            for k in range(NX):
                pf = k * (1 - c) + y * c
                ps = y * (1 - c) + k * c
                ref = whole_t.at[c, pf, ps]
                pairs.append(send(ref, ref, partner))
            eliminate(72, 128)

        diagonal = jnp.sum(
            jnp.where(
                lax.broadcasted_iota(jnp.int32, (COMP, COMP), 0)
                == lax.broadcasted_iota(jnp.int32, (COMP, COMP), 1),
                elim[...],
                0.0,
            ),
            axis=1,
            keepdims=True,
        )
        inverse = unit[...] * (1.0 / jnp.sqrt(diagonal))
        unit[...] = inverse
        inv_t[...] = inverse.T

        if not last:
            arrive([out_c])
            for pc in range(2):
                for pf in range(4):
                    for ps in range(4):
                        px, py = (pf, ps) if pc == 0 else (ps, pf)
                        col = (py * 8 + pc * 4 + px) * 128
                        value = jnp.dot(
                            unit[...],
                            whole_t[pc, pf, ps],
                            precision=HIGH,
                            preferred_element_type=jnp.float32,
                        )
                        basis_t[:, col : col + 128] = value.astype(jnp.bfloat16)
            for i in range(slabs):
                part = slice(i * SLAB, (i + 1) * SLAB)
                term = lax.dot_general(
                    stand[:, part],
                    basis_t[:, part],
                    (((1,), (1,)), ((), ())),
                    preferred_element_type=jnp.float32,
                )
                if i == 0:
                    acc[...] = term
                else:
                    acc[...] += term
        else:
            root = math.sqrt(kept_total)

            @pl.loop(0, n_kept // 128)
            def _(i):
                here = pl.ds(pl.multiple_of(i * 128, 128), 128)
                picks = jnp.broadcast_to(keep_ref[:, here], (128, 128)).T
                lane = lax.broadcasted_iota(jnp.int32, (128, 128), 1)
                one_hot = jnp.concatenate(
                    [
                        jnp.where(picks == lane + 128 * k, 1.0, 0.0).astype(
                            jnp.bfloat16
                        )
                        for k in range(rows // 128)
                    ],
                    axis=1,
                )
                chosen = jnp.dot(
                    one_hot, pm[...], preferred_element_type=jnp.float32
                )
                scores_ref[here, :] = (
                    jnp.dot(
                        chosen,
                        inv_t[...],
                        precision=HIGH,
                        preferred_element_type=jnp.float32,
                    )
                    * root
                )

            arrive(pairs)
            for pc in range(2):
                for k in range(NX):
                    if pc == 0:
                        value = whole_t[0, k, y]
                    else:
                        value = whole_t[1, y, k]
                    value = jnp.dot(
                        unit[...],
                        value,
                        precision=HIGH,
                        preferred_element_type=jnp.float32,
                    )
                    row0 = (pc * NX + k) * 128
                    load_ref[row0 : row0 + 128, :] = value.T

    for copy in sent:
        copy.wait_send()


def on_device(dosage, keep_rows, allele_counts, projection):
    groups = lax.axis_size("wide") * lax.axis_size("narrow")
    rows, snps = dosage.shape
    n_kept = keep_rows.shape[0]
    share = snps // lax.axis_size("narrow")
    f32, bf16 = jnp.float32, jnp.bfloat16
    vmem = pltpu.VMEM
    total_copies = 49 * ITERS

    def body(*refs):
        kernel(rows * groups, n_kept * groups, *refs)

    return pl.pallas_call(
        body,
        out_shape=(
            jax.ShapeDtypeStruct((n_kept, COMP), f32),
            jax.ShapeDtypeStruct((share, COMP), f32),
        ),
        in_specs=[
            pl.BlockSpec(memory_space=pl.ANY),
            pl.BlockSpec(memory_space=vmem),
            pl.BlockSpec(memory_space=vmem),
            pl.BlockSpec(memory_space=vmem),
        ],
        out_specs=(
            pl.BlockSpec(memory_space=vmem),
            pl.BlockSpec(memory_space=vmem),
        ),
        scratch_shapes=[
            vmem((rows, snps), bf16),
            vmem((rows, COMP), f32),
            vmem((rows, COMP), bf16),
            vmem((COMP, rows), bf16),
            vmem((rows, COMP), f32),
            vmem((ITERS, 2, 4, 4, COMP, 128), f32),
            vmem((ITERS, 4, 4, COMP, 128), f32),
            vmem((ITERS, 4, 4, COMP, 128), f32),
            vmem((ITERS, 3, 4, COMP, 128), f32),
            vmem((ITERS, 4, COMP, 128), f32),
            vmem((ITERS, 3, COMP, 128), f32),
            vmem((ITERS, COMP, 128), f32),
            vmem((ITERS, NZ - 1, 16, 128), f32),
            vmem((ITERS, 2, 4, 4, COMP, 128), f32),
            vmem((COMP, snps), bf16),
            vmem((ITERS, COMP, COMP), f32),
            vmem((ITERS, COMP, COMP), f32),
            vmem((ITERS, 64, COMP), f32),
            vmem((ITERS, NX, 16, COMP), f32),
            vmem((ITERS, NY, 16, COMP), f32),
            vmem((ITERS, NZ, 16, COMP), f32),
            vmem((ITERS, COMP, COMP), f32),
            vmem((COMP, COMP), f32),
            vmem((COMP, COMP), f32),
            vmem((COMP, COMP), f32),
            vmem((8, 128), f32),
            pltpu.SemaphoreType.DMA((snps // SLAB,)),
            pltpu.SemaphoreType.DMA((total_copies,)),
            pltpu.SemaphoreType.DMA((total_copies,)),
        ],
        compiler_params=pltpu.CompilerParams(
            collective_id=0, has_side_effects=True
        ),
    )(
        dosage,
        keep_rows.reshape(1, n_kept),
        allele_counts.reshape(1, snps),
        projection,
    )


def solution(mesh):
    in_specs = (P(("wide", "narrow"), None), P(("wide", "narrow")), P(), P())
    out_specs = (P(("wide", "narrow"), None), P("narrow", None))
    return jax.shard_map(
        on_device, mesh=mesh, in_specs=in_specs, out_specs=out_specs, check_vma=False
    )
```

time: 646 us -> 118 us (0.18)
  waiting for transfers between devices: 527 us -> 0 us
  Pallas kernels: 0 us -> 111 us
  other arithmetic: 56.2 us -> 0 us
  matrix products: 24.9 us -> 0 us
  local copies, waits for them, and re-layouts: 22.4 us -> 4.95 us
  between operations: 14.2 us -> 0.64 us
    psum x2 -> x0, waiting for transfers between devices: 527 us -> none  [the longest x1 267 us: on_device(): lax.psum(transposed_product(standard, projected), ('wide', 'narrow'))]
    pallas_call x0 -> x1, Pallas kernels: none -> 111 us  [on_device(): pl.pallas_call(body, out_shape=(jax.ShapeDtypeStruct((n_kept, COMP), f32)...]
    another operation x10 -> x0, other arithmetic: 45.7 us -> none  [the longest x6 24.8 us: invert_factor(): lower_factor = jnp.linalg.cholesky(gram_matrix)]
    dot_general x9 -> x0, matrix products: 24.3 us -> none  [the longest x4 8.84 us: transposed_product(): lax.dot_general(left_side, right_side, (((0,), (0,)), ((), ())), preferre...]
    gather x1 -> x0, local copies, waits for them, and re-layouts: 19.5 us -> none  [on_device(): chosen = jnp.take(dosage, keep_rows, axis=0)]
    convert_element_type x1 -> x0, other arithmetic: 6.56 us -> none  [on_device(): ((chosen.astype(jnp.float32) - center) / spread).astype(jnp.bfloat16)]
  transfers between devices with their start and end apart: 2 -> 0, of which waited for: 2 -> 0; matrix products, arithmetic and copies ran while one was open for 0% -> 0% of each run, Pallas kernels for 0% -> 0%
where the time goes in v1:
time: 118 us; the launch traced here: 117 us
  Pallas kernels  111 us (94%)
  local copies, waits for them, and re-layouts  4.95 us (4%)
    pallas_call x1, Pallas kernels, on_device(): pl.pallas_call(body, out_shape=(jax.ShapeDtypeStruct((n_kept, COMP), f32)...  111 us
    unnamed x2, local copies, waits for them, and re-layouts  3.68 us

profile of v1, /device:TPU:8, one launch (start us, length us, event | category | flops | bytes accessed | tf_op | source)
XLA Modules:
  0.0 116.8 jit_solution(17656905345816976437)
XLA Ops:
  0.6 1.3 %reshape.10.refs_1_ = s32[1,896]{1,0:T(1,128)} reshape(s32[896]{0:T(1024)} %param.5) | data formatting | bytes 7168 | tf_op jit(solution)/shard_map/reshape | solution.py:508
  1.9 111.2 %shard_map.59 = (f32[896,128]{1,0:T(8,128)}, f32[1024,128]{1,0:T(8,128)}) custom-call(bf16[1024,4096]{1,0:T(8,128)(2,1)} %refs_0_.1, s32[1,896]{1,0:T(1,128)} %reshape.10.refs_1_, s32[1,4096]{1,0:T(1,128)} %bitcast.1, bf16[4096,128]{1,0:T(8,128)(2,1)} %refs_3_.1), custom_call_target="tpu_custom_call" | custom-call | tf_op jit(solution)/shard_map/pallas_call | solution.py:456
  113.1 1.8 %copy.8 = f32[896,128]{1,0:T(8,128)} copy(f32[896,128]{1,0:T(8,128)} %get-tuple-element.4) | data formatting | bytes 917504
  114.9 1.9 %copy.9 = f32[1024,128]{1,0:T(8,128)} copy(f32[1024,128]{1,0:T(8,128)} %get-tuple-element.5) | data formatting | bytes 1048576
